TPU v7x, 128 devices: a whole 4x4x4 slice. The times are simulated.
128 devices in a mesh: dev: 128 (over x, y, z, core).
Axes of the slice: x: 4, y: 4, z: 4, core: 2. Of those that a mesh axis runs over, the one named last changes fastest.
Arguments:
- params: float32 [9, 131072], P(None, 'dev')
- moment: float32 [9, 131072], P(None, 'dev'), may hold values from -3 to 3
- second: float32 [9, 131072], P(None, 'dev'), may hold values from 0.05 to 1
- fetch_ids: int32 [128, 128, 8], P('dev'), may hold values from 0 to 1023
- seg_ids: int32 [512, 256], P('dev'), may hold values from 0 to 1023
- seg_count: int32 [512], P('dev'), may hold values from 1 to 256, 98304 in all
- seg_perm: int32 [512], replicated, may hold values from 0 to 511, as said below
- target: float32 [128, 3, 256], P('dev'), may hold values from 0 to 1
Outputs:
- image: float32 [128, 3, 256], P('dev')
- new_params: float32 [9, 131072], P(None, 'dev')
- new_moment: float32 [9, 131072], P(None, 'dev')
- new_second: float32 [9, 131072], P(None, 'dev')
Inputs may be any that keep to these rules, and one draw needn't show every extreme that they name: `seg_count`: segments that exceed their count hold unused slots; some segment is full. `seg_perm`: each number appears once.
All inputs are finite; a program needn't handle non-finite values. No bound on the sum of `seg_count` on one device may be relied on, other than what follows from the above.
Results may differ from a plain program's by a relative error of at most 0.0003.
Values sent between devices are 32-bit elements; how exact they have to be, the bound alone decides.
A program may use at most 192 MiB of HBM per device.

v0:
```python
import jax
import jax.numpy as jnp
from jax import lax
from jax.sharding import PartitionSpec as P

TILES_X = 8
KSEG = 4


def segment(par, count, tile):
    span = par.shape[1]
    pidx = jnp.arange(256, dtype=jnp.int32)
    fine_x = ((pidx % 16).astype(jnp.float32) + 0.5) / 16.0
    fine_y = ((pidx // 16).astype(jnp.float32) + 0.5) / 16.0
    pos_x = (tile % TILES_X).astype(jnp.float32) + fine_x
    pos_y = (tile // TILES_X).astype(jnp.float32) + fine_y
    steps = jnp.arange(span, dtype=jnp.int32)
    live = (steps < count).astype(jnp.float32)
    delta_x = pos_x[None, :] - par[0][:, None]
    delta_y = pos_y[None, :] - par[1][:, None]
    scale_a = jnp.exp(par[2])
    scale_c = jnp.exp(par[3])
    cross = 0.8 * jnp.tanh(par[4]) * scale_a * scale_c
    power = -0.5 * (
        (scale_a * scale_a)[:, None] * delta_x * delta_x
        + 2.0 * cross[:, None] * delta_x * delta_y
        + (scale_c * scale_c)[:, None] * delta_y * delta_y
    )
    alpha = (0.95 * jax.nn.sigmoid(par[5]) * live)[:, None] * jnp.exp(power)
    logt = jnp.log1p(-alpha)
    lower = (steps[:, None] > steps[None, :]).astype(jnp.float32)
    earlier = jnp.dot(lower, logt, precision=lax.Precision.HIGHEST)
    weight = jnp.exp(earlier) * alpha
    colour = jnp.dot(par[6:9], weight, precision=lax.Precision.HIGHEST)
    return (colour, jnp.sum(logt, axis=0))


def per_device(params, moment, second, fetch_ids, seg_ids, seg_count, seg_perm, target):
    ndev = lax.axis_size("dev")
    me = lax.axis_index("dev")
    nparam, owned = params.shape
    segs, span = seg_ids.shape
    tiles_dev = target.shape[0]
    pixels = target.shape[2]
    wanted = fetch_ids[0]
    cap = wanted.shape[1]
    received = lax.all_to_all(wanted, "dev", split_axis=0, concat_axis=0, tiled=True)
    buckets = jnp.take(params, received, axis=1)
    arrived = lax.all_to_all(buckets, "dev", split_axis=1, concat_axis=1, tiled=True)
    buffer = arrived.reshape(nparam, ndev * cap)
    first = me * segs
    own_perm = lax.dynamic_slice_in_dim(seg_perm, first, segs, 0)
    own_tile = own_perm // KSEG
    own_rank = own_perm % KSEG
    gathered_par = jnp.moveaxis(jnp.take(buffer, seg_ids, axis=1), 1, 0)

    def partials(values):
        return jax.vmap(segment)(values, seg_count, own_tile)

    (colours, logs), back = jax.vjp(partials, gathered_par)
    all_colours, all_logs, all_target = (
        lax.all_gather(colours, "dev", axis=0, tiled=True),
        lax.all_gather(logs, "dev", axis=0, tiled=True),
        lax.all_gather(target, "dev", axis=0, tiled=True),
    )
    total = all_logs.shape[0]
    ntiles = all_target.shape[0]
    tile_all = seg_perm // KSEG
    rank_all = seg_perm % KSEG
    same = tile_all[:, None] == tile_all[None, :]
    before = (same & (rank_all[None, :] < rank_all[:, None])).astype(jnp.float32)
    prefix = jnp.exp(jnp.dot(before, all_logs, precision=lax.Precision.HIGHEST))
    contrib = (prefix[:, None, :] * all_colours).reshape(total, 3 * pixels)
    onehot = (jnp.arange(ntiles, dtype=jnp.int32)[:, None] == tile_all[None, :]).astype(jnp.float32)
    image = jnp.dot(onehot, contrib, precision=lax.Precision.HIGHEST)
    misfit = image - all_target.reshape(ntiles, 3 * pixels)
    later = (
        (own_tile[:, None] == tile_all[None, :]) & (rank_all[None, :] > own_rank[:, None])
    ).astype(jnp.float32)
    behind = jnp.dot(later, contrib, precision=lax.Precision.HIGHEST).reshape(segs, 3, pixels)
    picker = (own_tile[:, None] == jnp.arange(ntiles, dtype=jnp.int32)[None, :]).astype(jnp.float32)
    error = jnp.dot(picker, misfit, precision=lax.Precision.HIGHEST).reshape(segs, 3, pixels)
    own_prefix = lax.dynamic_slice_in_dim(prefix, first, segs, 0)
    d_colour = own_prefix[:, None, :] * error
    d_log = jnp.sum(error * behind, axis=1)
    (d_par,) = back((d_colour, d_log))
    slot_grad = (
        jnp.zeros((nparam, ndev * cap), jnp.float32)
        .at[:, seg_ids.reshape(-1)]
        .add(jnp.moveaxis(d_par, 1, 0).reshape(nparam, segs * span))
    )
    returned = lax.all_to_all(
        slot_grad.reshape(nparam, ndev, cap), "dev", split_axis=1, concat_axis=1, tiled=True
    )
    grad = (
        jnp.zeros((nparam, owned), jnp.float32)
        .at[:, received.reshape(-1)]
        .add(returned.reshape(nparam, ndev * cap))
    )
    new_moment = 0.9 * moment + 0.1 * grad
    new_second = 0.99 * second + 0.01 * grad * grad
    new_params = params - 0.05 * new_moment / (jnp.sqrt(new_second) + 1e-08)
    my_image = lax.dynamic_slice_in_dim(image, me * tiles_dev, tiles_dev, 0).reshape(
        tiles_dev, 3, pixels
    )
    return (my_image, new_params, new_moment, new_second)


def solution(mesh):
    placed = (
        P(None, "dev"),
        P(None, "dev"),
        P(None, "dev"),
        P("dev", None, None),
        P("dev", None),
        P("dev"),
        P(),
        P("dev", None, None),
    )
    return jax.shard_map(
        per_device,
        mesh=mesh,
        in_specs=placed,
        out_specs=(P("dev", None, None), P(None, "dev"), P(None, "dev"), P(None, "dev")),
        check_vma=False,
    )
```

profile of v0, /device:TPU:1, one launch (start us, length us, event | category | flops | bytes accessed | tf_op | source)
XLA Modules:
  0.0 180.8 jit_solution(5734400977405865448)
XLA Ops:
  7.2 1.4 copy.73
  8.6 11.5 %all-to-all-start = ((s32[128,1,8]{2,1,0:T(1,128)}), s32[128,1,8]{2,1,0:T(1,128)S(1)}, u32[]{:S(2)}, u32[]{:S(2)}) async-start(s32[128,1,8]{2,1,0:T(1,128)} %bitcast), calls=%async_computation | async-start | bytes 131072 | tf_op jit(solution)/shard_map/all_to_all | solution.py:47
  20.1 0.7 fusion.92
  20.8 0.7 compare_and_fusion.1
  21.5 0.8 and_select_fusion
  22.3 0.8 fusion.102
  23.0 0.1 broadcast_add_fusion.1
  23.1 1.1 copy.74
  24.2 5.2 %all-to-all-done = s32[128,1,8]{2,1,0:T(1,128)S(1)} async-done(((s32[128,1,8]{2,1,0:T(1,128)}), s32[128,1,8]{2,1,0:T(1,128)S(1)}, u32[]{:S(2)}, u32[]{:S(2)}) %all-to-all-start) | async-done | bytes 4128 | tf_op jit(solution)/shard_map/all_to_all | solution.py:47
  29.4 0.1 reshape.400
  29.5 2.8 %gather_fusion = f32[1024,9]{1,0:T(8,128)S(1)} fusion(f32[9,1024]{0,1:T(8,128)S(1)} %copy.74, s32[1024]{0:T(1024)S(1)} %broadcast_clamp_fusion.1), kind=kCustom, calls=%fused_computation | custom fusion | bytes 77824 | tf_op jit(solution)/shard_map/jit(_take)/gather | solution.py:48
  32.4 1.0 fusion.43
  33.4 4.8 %all-to-all-start.1 = ((f32[9,128,8]{0,2,1:T(8,128)}), f32[9,128,8]{0,2,1:T(8,128)S(1)}, u32[]{:S(2)}, u32[]{:S(2)}) async-start(f32[9,128,8]{0,2,1:T(8,128)} %fusion.43), calls=%async_computation.1 | async-start | bytes 1048576 | tf_op jit(solution)/shard_map/all_to_all | solution.py:49
  38.2 13.5 %all-to-all-done.1 = f32[9,128,8]{0,2,1:T(8,128)S(1)} async-done(((f32[9,128,8]{0,2,1:T(8,128)}), f32[9,128,8]{0,2,1:T(8,128)S(1)}, u32[]{:S(2)}, u32[]{:S(2)}) %all-to-all-start.1) | async-done | bytes 36896 | tf_op jit(solution)/shard_map/all_to_all | solution.py:49
  51.7 2.8 %gather_fusion.1 = f32[1024,9]{1,0:T(8,128)S(1)} fusion(f32[9,1024]{0,1:T(8,128)S(1)} %bitcast.116, s32[1024]{0:T(1024)S(1)} %broadcast_clamp_fusion), kind=kCustom, calls=%fused_computation.1 | custom fusion | bytes 77824 | tf_op jit(solution)/shard_map/jit(_take)/gather | solution.py:55
  54.5 0.2 copy.76
  54.8 0.1 bitcast_select_fusion.1
  54.9 1.5 convolution_exponential_fusion
  56.4 2.1 %fusion.60 = f32[4,3,256]{2,1,0:T(4,128)} fusion(f32[256,4,256]{0,2,1:T(8,128)S(1)} %convolution_exponential_fusion, f32[4,256]{1,0:T(4,128)S(1)} %get-tuple-element.48, f32[4,256]{1,0:T(4,128)S(1)} %get-tuple-element.51, f32[4,256]{1,0:T(4,128)S(1)} %get-tuple-element.56, f32[4,256]{1,0:T(4,128)S(1)} %get-tuple-element.44, ...), kind=kOutput, calls=%fused_computation.86 | convolution fusion | flops 12845056 | bytes 1110016 | tf_op jit(solution)/shard_map/jvp(vmap())/dot_general | solution.py:34
  58.5 33.7 %all_gather.11 = f32[128,3,256]{2,1,0:T(4,128)S(1)} all-gather(f32[1,3,256]{2,1,0:T(4,128)S(1)} %copy.80), channel_id=1, replica_groups=mesh['dev'=128] {'dev'}, dimensions={0}, use_global_device_ids=true | all-gather | bytes 396288 | tf_op jit(solution)/shard_map/all_gather | solution.py:64
  92.3 0.2 copy.81
  92.5 0.2 copy.82
  92.7 0.5 broadcast.499
  93.2 0.8 reduce.3
  94.0 0.1 reshape.387
  94.1 1.0 log-plus-one_reduce_fusion
  95.2 35.5 %all-gather = f32[128,4,256]{2,1,0:T(4,128)S(1)} all-gather(f32[1,4,256]{2,1,0:T(4,128)S(1)} %bitcast.127), channel_id=1, replica_groups=mesh['dev'=128] {'dev'}, dimensions={0}, use_global_device_ids=true | all-gather | bytes 528384 | tf_op jit(solution)/shard_map/all_gather | solution.py:63
  130.7 0.2 reshape.434
  130.9 0.7 convolution_exponential_fusion.1
  131.6 0.2 copy.77
  131.9 1.8 %copy.79 = f32[512,3,256]{0,2,1:T(8,128)S(1)} copy(f32[512,3,256]{2,1,0:T(4,128)} %all-gather.3.cloned.1.call-done) | data formatting | bytes 3145728 | tf_op jit(solution)/shard_map/all_gather | solution.py:62
  133.7 0.2 broadcast_multiply_fusion
  133.9 1.0 fusion.66
  134.9 0.3 fusion.61
  135.2 1.1 fusion.72
  136.3 1.2 fusion.59
  137.5 0.8 fusion.12
  138.3 3.0 %fusion.33 = (f32[4,256]{1,0:T(4,128)S(1)}, f32[4,256]{1,0:T(4,128)S(1)}, f32[4,256]{1,0:T(4,128)S(1)}, f32[4,256]{1,0:T(4,128)S(1)}, f32[4,256]{1,0:T(4,128)S(1)}, /*index=5*/f32[4,256]{1,0:T(4,128)S(1)}) fusion(f32[4,256]{1,0:T(4,128)S(1)} %get-tuple-element.51, f32[4,256]{1,0:T(4,128)S(1)} %get-tuple-element.56, f32[4,256]{1,0:T(4,128)S(1)} %get-tuple-element.48, ...), kind=kOutput, calls=%fused_computation.52 | convolution fusion | flops 820570112 | bytes 2183168 | tf_op jit(solution)/shard_map/transpose(jvp(vmap()))/dot_general | solution.py:32
  141.4 0.1 fusion.81
  141.5 0.1 add_bitcast_fusion
  141.7 0.2 copy.87
  141.9 6.8 %scatter_custom_fusion = f32[9,1024]{0,1:T(8,128)} fusion(s32[1024]{0:T(1024)S(1)} %bitcast.130, f32[1024,9]{1,0:T(8,128)S(1)} %copy.87, f32[]{:T(128)} %constant.149.clone.1), kind=kCustom, calls=%fused_computation.90 | custom fusion | flops 9216 | bytes 36868 | tf_op jit(solution)/shard_map/scatter-add | solution.py:90
  148.7 4.6 %all-to-all-start.2 = ((f32[9,128,8]{0,2,1:T(8,128)}), f32[9,128,8]{0,2,1:T(8,128)S(1)}, u32[]{:S(2)}, u32[]{:S(2)}) async-start(f32[9,128,8]{0,2,1:T(8,128)} %bitcast.30), calls=%async_computation.2 | async-start | bytes 1048576 | tf_op jit(solution)/shard_map/all_to_all | solution.py:92
  153.4 0.6 constant_dynamic-slice_fusion.1
  154.0 13.0 %all-to-all-done.2 = f32[9,128,8]{0,2,1:T(8,128)S(1)} async-done(((f32[9,128,8]{0,2,1:T(8,128)}), f32[9,128,8]{0,2,1:T(8,128)S(1)}, u32[]{:S(2)}, u32[]{:S(2)}) %all-to-all-start.2) | async-done | bytes 36896 | tf_op jit(solution)/shard_map/all_to_all | solution.py:92
  166.9 6.2 %scatter_custom_fusion.1 = f32[9,1024]{0,1:T(8,128)S(1)} fusion(s32[1024]{0:T(1024)S(1)} %bitcast.129, f32[9,128,8]{0,2,1:T(8,128)S(1)} %all-to-all-done.2, f32[]{:T(128)} %constant.149.clone.1), kind=kCustom, calls=%fused_computation.67 | custom fusion | flops 9216 | bytes 561156 | tf_op jit(solution)/shard_map/scatter-add | solution.py:98
  173.1 0.2 copy.88
  173.3 0.7 divide_subtract_fusion
  (50 shorter events, 0.4 us)
Async XLA Ops:
  8.6 20.8 %all-to-all-start = ((s32[128,1,8]{2,1,0:T(1,128)}), s32[128,1,8]{2,1,0:T(1,128)S(1)}, u32[]{:S(2)}, u32[]{:S(2)}) async-start(s32[128,1,8]{2,1,0:T(1,128)} %bitcast), calls=%async_computation | async-start | bytes 131072 | tf_op jit(solution)/shard_map/all_to_all | solution.py:47
  32.3 22.4 %copy-start.6 = (s32[4]{0:T(128)S(1)}, s32[4]{0:T(128)}, u32[]{:S(2)}) copy-start(s32[4]{0:T(128)} %param.13) | copy-start | bytes 52
  33.4 18.3 %all-to-all-start.1 = ((f32[9,128,8]{0,2,1:T(8,128)}), f32[9,128,8]{0,2,1:T(8,128)S(1)}, u32[]{:S(2)}, u32[]{:S(2)}) async-start(f32[9,128,8]{0,2,1:T(8,128)} %fusion.43), calls=%async_computation.1 | async-start | bytes 1048576 | tf_op jit(solution)/shard_map/all_to_all | solution.py:49
  38.1 93.7 %all-gather.3.cloned.1.call-start = ((), (), s32[]{:S(2)}) async-start(), calls=%async_computation.3 | async-start | bytes 2113536 | tf_op jit(solution)/shard_map/all_gather | solution.py:62
  56.3 2.1 %copy-start.7 = (f32[256,4,256]{0,2,1:T(8,128)}, f32[256,4,256]{0,2,1:T(8,128)S(1)}, u32[]{:S(2)}) copy-start(f32[256,4,256]{0,2,1:T(8,128)S(1)} %convolution_exponential_fusion) | copy-start | bytes 3145732
  56.3 2.2 %copy-start.3 = (s32[4,256]{1,0:T(4,128)S(1)}, s32[4,256]{1,0:T(4,128)}, u32[]{:S(2)}) copy-start(s32[4,256]{1,0:T(4,128)} %param.12) | copy-start | bytes 12292
  56.4 2.2 %copy-start.5 = (f32[1,3,256]{2,0,1:T(1,128)S(1)}, f32[1,3,256]{2,0,1:T(1,128)}, u32[]{:S(2)}) copy-start(f32[1,3,256]{2,0,1:T(1,128)} %param.15) | copy-start | bytes 9220
  58.5 34.2 %copy-start.4 = (s32[512]{0:T(512)S(1)}, s32[512]{0:T(512)}, u32[]{:S(2)}) copy-start(s32[512]{0:T(512)} %param.14) | copy-start | bytes 6148
  133.9 2.4 %copy-start.8 = (f32[256,4,256]{0,2,1:T(8,128)S(1)}, f32[256,4,256]{0,2,1:T(8,128)}, u32[]{:S(2)}) copy-start(f32[256,4,256]{0,2,1:T(8,128)} %copy-done.7) | copy-start | bytes 3145732
  141.9 31.4 %copy-start = (f32[9,1024]{1,0:T(8,128)S(1)}, f32[9,1024]{1,0:T(8,128)}, u32[]{:S(2)}) copy-start(f32[9,1024]{1,0:T(8,128)} %param.8) | copy-start | bytes 110596
  141.9 31.4 %copy-start.1 = (f32[9,1024]{1,0:T(8,128)S(1)}, f32[9,1024]{1,0:T(8,128)}, u32[]{:S(2)}) copy-start(f32[9,1024]{1,0:T(8,128)} %param.9) | copy-start | bytes 110596
  141.9 31.4 %copy-start.2 = (f32[9,1024]{1,0:T(8,128)S(1)}, f32[9,1024]{1,0:T(8,128)}, u32[]{:S(2)}) copy-start(f32[9,1024]{1,0:T(8,128)} %param.10) | copy-start | bytes 110596
  148.7 18.2 %all-to-all-start.2 = ((f32[9,128,8]{0,2,1:T(8,128)}), f32[9,128,8]{0,2,1:T(8,128)S(1)}, u32[]{:S(2)}, u32[]{:S(2)}) async-start(f32[9,128,8]{0,2,1:T(8,128)} %bitcast.30), calls=%async_computation.2 | async-start | bytes 1048576 | tf_op jit(solution)/shard_map/all_to_all | solution.py:92
Sparse Core Ops, SparseCore 0:
  58.6 62.3 all-gather.2
where the time goes:
time: 181 us
  blocking collectives  69.2 us (38%)
  waiting for transfers between devices  31.7 us (18%)
  starting transfers between devices  20.9 us (12%)
  other arithmetic  20.1 us (11%)
  between operations  14.5 us (8%)
  local copies, waits for them, and re-layouts  12.7 us (7%)
  matrix products  11.7 us (6%)
    all_gather x1, blocking collectives, per_device(): lax.all_gather(logs, 'dev', axis=0, tiled=True)  35.5 us
    all_gather x1, blocking collectives, per_device(): lax.all_gather(target, 'dev', axis=0, tiled=True)  33.7 us
    all_to_all x1, waiting for transfers between devices, per_device(): lax.all_to_all(buckets, 'dev', split_axis=1, concat_axis=1, tiled=True)  13.5 us
    all_to_all x1, waiting for transfers between devices, per_device(): lax.all_to_all(slot_grad.reshape(nparam, ndev, cap), 'dev', split_axis=1,...  13 us
    all_to_all x1, starting transfers between devices, per_device(): lax.all_to_all(wanted, 'dev', split_axis=0, concat_axis=0, tiled=True)  11.5 us
    scatter-add x1, other arithmetic, per_device(): slot_grad = jnp.zeros((nparam, ndev * cap), jnp.float32).at[:, seg_ids.re...  6.79 us
    scatter-add x1, other arithmetic, per_device(): grad = jnp.zeros((nparam, owned), jnp.float32).at[:, received.reshape(-1)...  6.18 us
    all_to_all x1, waiting for transfers between devices, per_device(): lax.all_to_all(wanted, 'dev', split_axis=0, concat_axis=0, tiled=True)  5.21 us
  transfers between devices with their start and end apart: 4, of which 3 were waited for; matrix products, arithmetic and copies ran while one was open for 5% of the time, Pallas kernels for 0%

commit v1 on v0

--- a/solution.py
+++ b/solution.py
@@ -5,6 +5,13 @@
 
 TILES_X = 8
 KSEG = 4
+
+
+def all_by_exchange(block, axis, along):
+    size = lax.axis_size(axis)
+    blocks = jnp.stack([block for _ in range(size)])
+    blocks = lax.all_to_all(blocks, axis, split_axis=0, concat_axis=0)
+    return jnp.concatenate(blocks, axis=along)
 
 
 def segment(par, count, tile):
@@ -61,7 +68,7 @@
     all_colours, all_logs, all_target = (
         lax.all_gather(colours, "dev", axis=0, tiled=True),
         lax.all_gather(logs, "dev", axis=0, tiled=True),
-        lax.all_gather(target, "dev", axis=0, tiled=True),
+        all_by_exchange(target, "dev", 0),
     )
     total = all_logs.shape[0]
     ntiles = all_target.shape[0]

time: 181 us -> 173 us (0.956)
  blocking collectives: 69.2 us -> 38 us
  waiting for transfers between devices: 31.7 us -> 47.8 us
  starting transfers between devices: 20.9 us -> 26.3 us
    all_gather x1 -> x0, blocking collectives: 33.7 us -> none  [per_device(): lax.all_gather(target, 'dev', axis=0, tiled=True)]
    all_gather x1, waiting for transfers between devices: 0.02 us -> 16.1 us  [per_device(): lax.all_gather(colours, 'dev', axis=0, tiled=True)]
    all_to_all x0 -> x1, starting transfers between devices: none -> 4.71 us  [all_by_exchange(): blocks = lax.all_to_all(blocks, axis, split_axis=0, concat_axis=0)]
    all_gather x1, blocking collectives: 35.5 us -> 38 us  [per_device(): lax.all_gather(logs, 'dev', axis=0, tiled=True)]
  transfers between devices with their start and end apart: 4 -> 5, of which waited for: 3 -> 4; matrix products, arithmetic and copies ran while one was open for 5% -> 6% of each run, Pallas kernels for 0% -> 0%
where the time goes in v1:
time: 173 us; the launch traced here: 172 us
  waiting for transfers between devices  47.8 us (28%)
  blocking collectives  38 us (22%)
  starting transfers between devices  26.3 us (15%)
  other arithmetic  20.1 us (12%)
  between operations  14.5 us (8%)
  local copies, waits for them, and re-layouts  14 us (8%)
  matrix products  11.7 us (7%)
    all_gather x1, blocking collectives, per_device(): lax.all_gather(logs, 'dev', axis=0, tiled=True)  38 us
    all_gather x1, waiting for transfers between devices, per_device(): lax.all_gather(colours, 'dev', axis=0, tiled=True)  16.1 us
    all_to_all x1, waiting for transfers between devices, per_device(): lax.all_to_all(buckets, 'dev', split_axis=1, concat_axis=1, tiled=True)  13.5 us
    all_to_all x1, waiting for transfers between devices, per_device(): lax.all_to_all(slot_grad.reshape(nparam, ndev, cap), 'dev', split_axis=1,...  13 us
    all_to_all x1, starting transfers between devices, per_device(): lax.all_to_all(wanted, 'dev', split_axis=0, concat_axis=0, tiled=True)  11.5 us
    scatter-add x1, other arithmetic, per_device(): slot_grad = jnp.zeros((nparam, ndev * cap), jnp.float32).at[:, seg_ids.re...  6.79 us
    scatter-add x1, other arithmetic, per_device(): grad = jnp.zeros((nparam, owned), jnp.float32).at[:, received.reshape(-1)...  6.18 us
    all_to_all x1, starting transfers between devices, per_device(): lax.all_to_all(slot_grad.reshape(nparam, ndev, cap), 'dev', split_axis=1,...  5.32 us
  transfers between devices with their start and end apart: 5, of which 4 were waited for; matrix products, arithmetic and copies ran while one was open for 6% of the time, Pallas kernels for 0%

profile of v1, /device:TPU:1, one launch (start us, length us, event | category | flops | bytes accessed | tf_op | source)
XLA Modules:
  0.0 172.4 jit_solution(5935603426681092728)
XLA Ops:
  7.2 1.4 copy.92
  8.6 11.5 %all-to-all-start = ((s32[128,1,8]{2,1,0:T(1,128)}), s32[128,1,8]{2,1,0:T(1,128)S(1)}, u32[]{:S(2)}, u32[]{:S(2)}) async-start(s32[128,1,8]{2,1,0:T(1,128)} %bitcast), calls=%async_computation | async-start | bytes 131072 | tf_op jit(solution)/shard_map/all_to_all | solution.py:54
  20.1 0.7 fusion.92
  20.8 0.7 compare_and_fusion.1
  21.5 0.8 and_select_fusion
  22.3 0.8 fusion.102
  23.1 1.1 copy.93
  24.2 5.2 %all-to-all-done = s32[128,1,8]{2,1,0:T(1,128)S(1)} async-done(((s32[128,1,8]{2,1,0:T(1,128)}), s32[128,1,8]{2,1,0:T(1,128)S(1)}, u32[]{:S(2)}, u32[]{:S(2)}) %all-to-all-start) | async-done | bytes 4128 | tf_op jit(solution)/shard_map/all_to_all | solution.py:54
  29.4 0.1 reshape.399
  29.5 2.8 %gather_fusion = f32[1024,9]{1,0:T(8,128)S(1)} fusion(f32[9,1024]{0,1:T(8,128)S(1)} %copy.93, s32[1024]{0:T(1024)S(1)} %broadcast_clamp_fusion.1), kind=kCustom, calls=%fused_computation | custom fusion | bytes 77824 | tf_op jit(solution)/shard_map/jit(_take)/gather | solution.py:55
  32.4 1.0 fusion.43
  33.4 4.8 %all-to-all-start.1 = ((f32[9,128,8]{0,2,1:T(8,128)}), f32[9,128,8]{0,2,1:T(8,128)S(1)}, u32[]{:S(2)}, u32[]{:S(2)}) async-start(f32[9,128,8]{0,2,1:T(8,128)} %fusion.43), calls=%async_computation.1 | async-start | bytes 1048576 | tf_op jit(solution)/shard_map/all_to_all | solution.py:56
  38.2 13.5 %all-to-all-done.1 = f32[9,128,8]{0,2,1:T(8,128)S(1)} async-done(((f32[9,128,8]{0,2,1:T(8,128)}), f32[9,128,8]{0,2,1:T(8,128)S(1)}, u32[]{:S(2)}, u32[]{:S(2)}) %all-to-all-start.1) | async-done | bytes 36896 | tf_op jit(solution)/shard_map/all_to_all | solution.py:56
  51.7 2.8 %gather_fusion.1 = f32[1024,9]{1,0:T(8,128)S(1)} fusion(f32[9,1024]{0,1:T(8,128)S(1)} %bitcast.119, s32[1024]{0:T(1024)S(1)} %broadcast_clamp_fusion), kind=kCustom, calls=%fused_computation.1 | custom fusion | bytes 77824 | tf_op jit(solution)/shard_map/jit(_take)/gather | solution.py:62
  54.5 0.2 copy.95
  54.8 0.1 bitcast_select_fusion.1
  54.9 1.5 convolution_exponential_fusion
  56.4 2.1 %fusion.60 = f32[4,3,256]{2,1,0:T(4,128)} fusion(f32[256,4,256]{0,2,1:T(8,128)S(1)} %convolution_exponential_fusion, f32[4,256]{1,0:T(4,128)S(1)} %get-tuple-element.52, f32[4,256]{1,0:T(4,128)S(1)} %get-tuple-element.55, f32[4,256]{1,0:T(4,128)S(1)} %get-tuple-element.60, f32[4,256]{1,0:T(4,128)S(1)} %get-tuple-element.48, ...), kind=kOutput, calls=%fused_computation.86 | convolution fusion | flops 12845056 | bytes 1110016 | tf_op jit(solution)/shard_map/jvp(vmap())/dot_general | solution.py:41
  58.5 0.9 stack.2
  59.5 4.7 %all-to-all-start.2 = ((f32[128,1,3,256]{3,1,2,0:T(1,128)}), f32[128,1,3,256]{3,1,2,0:T(1,128)S(1)}, u32[]{:S(2)}, u32[]{:S(2)}) async-start(f32[128,1,3,256]{3,1,2,0:T(1,128)} %stack.2), calls=%async_computation.2 | async-start | bytes 786432 | tf_op jit(solution)/shard_map/all_to_all | solution.py:13
  64.3 0.5 broadcast.502
  64.8 0.8 reduce.3
  65.6 0.1 reshape.387
  65.7 1.0 log-plus-one_reduce_fusion
  66.7 38.0 %all-gather = f32[128,4,256]{2,1,0:T(4,128)S(1)} all-gather(f32[1,4,256]{2,1,0:T(4,128)S(1)} %bitcast.131), channel_id=1, replica_groups=mesh['dev'=128] {'dev'}, dimensions={0}, use_global_device_ids=true | all-gather | bytes 528384 | tf_op jit(solution)/shard_map/all_gather | solution.py:70
  104.7 0.2 reshape.433
  104.9 0.7 convolution_exponential_fusion.1
  105.6 0.2 copy.96
  105.9 0.6 copy.99
  106.5 0.2 copy.100
  106.6 16.1 %all-gather.3.cloned.1.call-done = f32[512,3,256]{2,1,0:T(4,128)} async-done(((f32[4,3,256]{2,1,0:T(4,128)}), f32[512,3,256]{2,1,0:T(4,128)}) %all-gather.3.cloned.1.call-update) | async-done | bytes 1572880 | tf_op jit(solution)/shard_map/all_gather | solution.py:69
  122.7 1.8 %copy.98 = f32[512,3,256]{0,2,1:T(8,128)S(1)} copy(f32[512,3,256]{2,1,0:T(4,128)} %all-gather.3.cloned.1.call-done) | data formatting | bytes 3145728 | tf_op jit(solution)/shard_map/all_gather | solution.py:69
  124.5 0.2 broadcast_multiply_fusion
  124.8 1.0 fusion.66
  125.8 0.3 fusion.61
  126.1 1.1 fusion.72
  127.1 1.2 fusion.59
  128.3 0.8 fusion.12
  129.2 3.0 %fusion.33 = (f32[4,256]{1,0:T(4,128)S(1)}, f32[4,256]{1,0:T(4,128)S(1)}, f32[4,256]{1,0:T(4,128)S(1)}, f32[4,256]{1,0:T(4,128)S(1)}, f32[4,256]{1,0:T(4,128)S(1)}, /*index=5*/f32[4,256]{1,0:T(4,128)S(1)}) fusion(f32[4,256]{1,0:T(4,128)S(1)} %get-tuple-element.55, f32[4,256]{1,0:T(4,128)S(1)} %get-tuple-element.60, f32[4,256]{1,0:T(4,128)S(1)} %get-tuple-element.52, ...), kind=kOutput, calls=%fused_computation.52 | convolution fusion | flops 820570112 | bytes 2183168 | tf_op jit(solution)/shard_map/transpose(jvp(vmap()))/dot_general | solution.py:39
  132.3 0.1 fusion.81
  132.5 0.2 copy.105
  132.8 6.8 %scatter_custom_fusion = f32[9,1024]{0,1:T(8,128)} fusion(s32[1024]{0:T(1024)S(1)} %bitcast.134, f32[1024,9]{1,0:T(8,128)S(1)} %copy.105, f32[]{:T(128)} %constant.149.clone.1), kind=kCustom, calls=%fused_computation.90 | custom fusion | flops 9216 | bytes 36868 | tf_op jit(solution)/shard_map/scatter-add | solution.py:97
  139.6 5.3 %all-to-all-start.3 = ((f32[9,128,8]{0,2,1:T(8,128)}), f32[9,128,8]{0,2,1:T(8,128)S(1)}, u32[]{:S(2)}, u32[]{:S(2)}) async-start(f32[9,128,8]{0,2,1:T(8,128)} %bitcast.30), calls=%async_computation.3 | async-start | bytes 1048576 | tf_op jit(solution)/shard_map/all_to_all | solution.py:99
  144.9 0.6 constant_dynamic-slice_fusion.1
  145.5 13.0 %all-to-all-done.3 = f32[9,128,8]{0,2,1:T(8,128)S(1)} async-done(((f32[9,128,8]{0,2,1:T(8,128)}), f32[9,128,8]{0,2,1:T(8,128)S(1)}, u32[]{:S(2)}, u32[]{:S(2)}) %all-to-all-start.3) | async-done | bytes 36896 | tf_op jit(solution)/shard_map/all_to_all | solution.py:99
  158.5 6.2 %scatter_custom_fusion.1 = f32[9,1024]{0,1:T(8,128)S(1)} fusion(s32[1024]{0:T(1024)S(1)} %bitcast.133, f32[9,128,8]{0,2,1:T(8,128)S(1)} %all-to-all-done.3, f32[]{:T(128)} %constant.149.clone.1), kind=kCustom, calls=%fused_computation.67 | custom fusion | flops 9216 | bytes 561156 | tf_op jit(solution)/shard_map/scatter-add | solution.py:105
  164.6 0.2 copy.106
  164.9 0.7 divide_subtract_fusion
  (52 shorter events, 0.5 us)
Async XLA Ops:
  8.6 20.8 %all-to-all-start = ((s32[128,1,8]{2,1,0:T(1,128)}), s32[128,1,8]{2,1,0:T(1,128)S(1)}, u32[]{:S(2)}, u32[]{:S(2)}) async-start(s32[128,1,8]{2,1,0:T(1,128)} %bitcast), calls=%async_computation | async-start | bytes 131072 | tf_op jit(solution)/shard_map/all_to_all | solution.py:54
  32.3 22.4 %copy-start.6 = (s32[4]{0:T(128)S(1)}, s32[4]{0:T(128)}, u32[]{:S(2)}) copy-start(s32[4]{0:T(128)} %param.13) | copy-start | bytes 52
  33.4 18.3 %all-to-all-start.1 = ((f32[9,128,8]{0,2,1:T(8,128)}), f32[9,128,8]{0,2,1:T(8,128)S(1)}, u32[]{:S(2)}, u32[]{:S(2)}) async-start(f32[9,128,8]{0,2,1:T(8,128)} %fusion.43), calls=%async_computation.1 | async-start | bytes 1048576 | tf_op jit(solution)/shard_map/all_to_all | solution.py:56
  38.1 84.6 %all-gather.3.cloned.1.call-start = ((), (), s32[]{:S(2)}) async-start(), calls=%async_computation.4 | async-start | bytes 2113536 | tf_op jit(solution)/shard_map/all_gather | solution.py:69
  56.3 2.1 %copy-start.7 = (f32[256,4,256]{0,2,1:T(8,128)}, f32[256,4,256]{0,2,1:T(8,128)S(1)}, u32[]{:S(2)}) copy-start(f32[256,4,256]{0,2,1:T(8,128)S(1)} %convolution_exponential_fusion) | copy-start | bytes 3145732
  56.3 2.2 %copy-start.5 = (f32[1,3,256]{2,0,1:T(1,128)S(1)}, f32[1,3,256]{2,0,1:T(1,128)}, u32[]{:S(2)}) copy-start(f32[1,3,256]{2,0,1:T(1,128)} %param.15) | copy-start | bytes 9220
  56.4 7.8 %copy-start.3 = (s32[4,256]{1,0:T(4,128)S(1)}, s32[4,256]{1,0:T(4,128)}, u32[]{:S(2)}) copy-start(s32[4,256]{1,0:T(4,128)} %param.12) | copy-start | bytes 12292
  56.4 7.9 %copy-start.4 = (s32[512]{0:T(512)S(1)}, s32[512]{0:T(512)}, u32[]{:S(2)}) copy-start(s32[512]{0:T(512)} %param.14) | copy-start | bytes 6148
  59.5 46.4 %all-to-all-start.2 = ((f32[128,1,3,256]{3,1,2,0:T(1,128)}), f32[128,1,3,256]{3,1,2,0:T(1,128)S(1)}, u32[]{:S(2)}, u32[]{:S(2)}) async-start(f32[128,1,3,256]{3,1,2,0:T(1,128)} %stack.2), calls=%async_computation.2 | async-start | bytes 786432 | tf_op jit(solution)/shard_map/all_to_all | solution.py:13
  124.8 2.4 %copy-start.8 = (f32[256,4,256]{0,2,1:T(8,128)S(1)}, f32[256,4,256]{0,2,1:T(8,128)}, u32[]{:S(2)}) copy-start(f32[256,4,256]{0,2,1:T(8,128)} %copy-done.7) | copy-start | bytes 3145732
  132.8 32.1 %copy-start = (f32[9,1024]{1,0:T(8,128)S(1)}, f32[9,1024]{1,0:T(8,128)}, u32[]{:S(2)}) copy-start(f32[9,1024]{1,0:T(8,128)} %param.8) | copy-start | bytes 110596
  132.8 32.1 %copy-start.1 = (f32[9,1024]{1,0:T(8,128)S(1)}, f32[9,1024]{1,0:T(8,128)}, u32[]{:S(2)}) copy-start(f32[9,1024]{1,0:T(8,128)} %param.9) | copy-start | bytes 110596
  132.8 32.1 %copy-start.2 = (f32[9,1024]{1,0:T(8,128)S(1)}, f32[9,1024]{1,0:T(8,128)}, u32[]{:S(2)}) copy-start(f32[9,1024]{1,0:T(8,128)} %param.10) | copy-start | bytes 110596
  139.6 18.9 %all-to-all-start.3 = ((f32[9,128,8]{0,2,1:T(8,128)}), f32[9,128,8]{0,2,1:T(8,128)S(1)}, u32[]{:S(2)}, u32[]{:S(2)}) async-start(f32[9,128,8]{0,2,1:T(8,128)} %bitcast.30), calls=%async_computation.3 | async-start | bytes 1048576 | tf_op jit(solution)/shard_map/all_to_all | solution.py:99
Sparse Core Ops, SparseCore 0:
  58.6 64.0 all-gather.2
